TPU v7x, 256 devices: a whole 4x4x8 slice. The times are simulated.
256 devices in a mesh: row: 16 (over x, z_lo, core), col: 16 (over z_hi, y).
Axes of the slice: x: 4, y: 4, z: 8 (z_hi: 4, z_lo: 2; z = z_hi * 2 + z_lo), core: 2. Of those that a mesh axis runs over, the one named last changes fastest.
Arguments:
- coefs: bfloat16 [1024, 16384], P('col', 'row'), may hold values from -6 to 6
- direction: bfloat16 [1024, 16384], P('col', 'row'), may hold values from -6 to 6
- tiles: bfloat16 [16, 384, 4096], P('row', 'col'), may hold values from -0.21875 to 0.21875
- block_rows: int32 [16, 384], P('row', 'col'), may hold values from 0 to 15
- block_cols: int32 [16, 384], P('row', 'col'), may hold values from 0 to 255
- counts: int32 [16, 16], P('row', 'col'), may hold values from 3 to 24, as said below
Outputs:
- h_coefs: bfloat16 [1024, 16384], P('col', 'row')
- h_direction: bfloat16 [1024, 16384], P('col', 'row')
Inputs may be any that keep to these rules, and one draw needn't show every extreme that they name: `counts`: each value lies between 3 and 24; some device's list is full in every draw. `block_cols`: tiles of one device may repeat a place.
All inputs are finite; a program needn't handle non-finite values.
Results may differ from a plain program's by a relative error of at most 0.008.
Values may be sent and summed in bfloat16 or wider, within the bound.
No kernel may reach another device: no remote copies, remote signals or barrier semaphores. Data moves between devices by JAX's collectives and lax.ppermute only.
A program may use at most 128 MiB of HBM per device.

v0:
```python
import jax
import jax.numpy as jnp
from jax import lax
from jax.sharding import PartitionSpec as P

BLOCK = 64


def make_folder(panels, row_blocks, total, piece):
    targets = lax.iota(jnp.int32, row_blocks)
    tile_flat, tile_rows, tile_cols = piece
    amount = tile_flat.shape[0]
    tile_mats = tile_flat.reshape(amount, BLOCK, BLOCK)
    picked = jnp.take(panels, tile_cols, axis=2)
    contrib = jnp.einsum("pij,sopj->psoi", tile_mats, picked, preferred_element_type=jnp.float32)
    contrib = contrib.reshape(amount, -1)
    upper = contrib.astype(jnp.bfloat16)
    lower = (contrib - upper.astype(jnp.float32)).astype(jnp.bfloat16)
    placing = (targets[:, None] == tile_rows[None, :]).astype(jnp.bfloat16)
    total = jnp.dot(placing, upper, preferred_element_type=jnp.float32)
    return total + jnp.dot(placing, lower, preferred_element_type=jnp.float32)


def finish(total, stacked, orbitals, row_blocks):
    shaped = total.reshape(row_blocks, stacked, orbitals, BLOCK).transpose(1, 2, 0, 3)
    return shaped.reshape(stacked, orbitals, row_blocks * BLOCK).astype(jnp.bfloat16)


def local(coefs, direction, tiles, block_rows, block_cols, counts):
    slots = tiles.shape[1]
    orbitals = coefs.shape[0]
    row_blocks = coefs.shape[1] // BLOCK
    slot_ids = lax.iota(jnp.int32, slots)
    used = (slot_ids < counts[0, 0]).astype(jnp.bfloat16)
    tile_flat = tiles[0] * used[:, None]
    rows_local = block_rows[0]
    cols_global = block_cols[0]
    whole_coefs, whole_direction = (
        lax.all_gather(coefs, "row", axis=1, tiled=True),
        lax.all_gather(direction, "row", axis=1, tiled=True),
    )
    all_blocks = whole_coefs.shape[1] // BLOCK
    coef_panel = whole_coefs.reshape(1, orbitals, all_blocks, BLOCK)
    direction_panel = whole_direction.reshape(1, orbitals, all_blocks, BLOCK)
    start_one = jnp.zeros((row_blocks, orbitals * BLOCK), jnp.float32)
    first_total = make_folder(
        coef_panel,
        row_blocks,
        start_one,
        (
            lax.all_gather(tile_flat, "col", axis=0, tiled=True),
            lax.all_gather(rows_local, "col", axis=0, tiled=True),
            lax.all_gather(cols_global, "col", axis=0, tiled=True),
        ),
    )
    second_total = make_folder(
        direction_panel,
        row_blocks,
        start_one,
        (
            lax.all_gather(tile_flat, "col", axis=0, tiled=True),
            lax.all_gather(rows_local, "col", axis=0, tiled=True),
            lax.all_gather(cols_global, "col", axis=0, tiled=True),
        ),
    )
    return (
        finish(first_total, 1, orbitals, row_blocks)[0],
        finish(second_total, 1, orbitals, row_blocks)[0],
    )


def solution(mesh):
    return jax.shard_map(
        local,
        mesh=mesh,
        in_specs=(
            P("col", "row"),
            P("col", "row"),
            P("row", "col", None),
            P("row", "col"),
            P("row", "col"),
            P("row", "col"),
        ),
        out_specs=(P("col", "row"), P("col", "row")),
        check_vma=False,
    )
```

profile of v0, /device:TPU:1, one launch (start us, length us, event | category | flops | bytes accessed | tf_op | source)
XLA Modules:
  0.0 238.3 jit_solution(10009733830007817194)
XLA Ops:
  7.2 0.0 all-gather.10.cloned.1.call-start
  7.2 0.7 all-gather.10.cloned.1.call-update
  7.9 0.0 all-gather.6.cloned.1.call-start
  7.9 0.7 all-gather.6.cloned.1.call-update
  8.6 0.0 all-gather.8.cloned.1.call-start
  9.4 1.7 bitcast_multiply_fusion
  11.0 0.0 all-gather.8.cloned.1.call-update
  11.1 1.3 dynamic-slice
  13.0 0.8 bitcast_dynamic-update-slice_fusion
  13.7 0.7 bitcast_dynamic-update-slice_fusion.1
  14.5 18.1 %all-reduce.2 = (s32[384]{0:T(512)S(1)}, s32[384]{0:T(512)S(1)}) all-reduce(s32[384]{0:T(512)S(1)} %bitcast_dynamic-update-slice_fusion, s32[384]{0:T(512)S(1)} %bitcast_dynamic-update-slice_fusion.1), channel_id=3, replica_groups=mesh['row'=16,'col'=16] {'col'}, use_global_device_ids=true, to_apply=%add.1 | all-reduce | flops 768 | bytes 6144 | tf_op jit(solution)/shard_map/all_gather | solution.py:53
  32.6 17.7 %all-gather.10.cloned.1.call-done = bf16[64,16384]{1,0:T(8,128)(2,1)} async-done(((bf16[64,1024]{1,0:T(8,128)(2,1)}), bf16[64,16384]{1,0:T(8,128)(2,1)}) %all-gather.10.cloned.1.call-update) | async-done | bytes 2097168 | tf_op jit(solution)/shard_map/all_gather | solution.py:40
  50.3 6.5 %reshape.69 = bf16[1,64,256,64]{3,2,1,0:T(8,128)(2,1)} reshape(bf16[64,16384]{1,0:T(8,128)(2,1)} %all-gather.10.cloned.1.call-done) | data formatting | bytes 4194304 | tf_op jit(solution)/shard_map/reshape | solution.py:44
  56.8 6.8 %copy.30 = bf16[1,64,256,64]{3,1,2,0:T(8,128)(2,1)} copy(bf16[1,64,256,64]{3,2,1,0:T(8,128)(2,1)} %reshape.69) | data formatting | bytes 4194304 | tf_op jit(solution)/shard_map/reshape | solution.py:44
  63.6 24.6 %all-gather.6.cloned.1.call-done = bf16[64,16384]{1,0:T(8,128)(2,1)} async-done(((bf16[64,1024]{1,0:T(8,128)(2,1)}), bf16[64,16384]{1,0:T(8,128)(2,1)}) %all-gather.6.cloned.1.call-update) | async-done | bytes 2097168 | tf_op jit(solution)/shard_map/all_gather | solution.py:39
  88.3 6.5 %reshape.65 = bf16[1,64,256,64]{3,2,1,0:T(8,128)(2,1)} reshape(bf16[64,16384]{1,0:T(8,128)(2,1)} %all-gather.6.cloned.1.call-done) | data formatting | bytes 4194304 | tf_op jit(solution)/shard_map/reshape | solution.py:43
  94.8 6.9 %copy.31 = bf16[1,64,256,64]{3,1,2,0:T(8,128)(2,1)} copy(bf16[1,64,256,64]{3,2,1,0:T(8,128)(2,1)} %reshape.65) | data formatting | bytes 4194304 | tf_op jit(solution)/shard_map/reshape | solution.py:43
  101.7 6.4 %gather_fusion.1 = bf16[384,64,64]{2,1,0:T(8,128)(2,1)} fusion(bf16[64,256,64]{2,0,1:T(8,128)(2,1)} %bitcast.60, s32[1024]{0:T(1024)S(1)} %pad_clamp_fusion), kind=kCustom, calls=%fused_computation.1.clone | custom fusion | bytes 6292992 | tf_op jit(solution)/shard_map/jit(_take)/gather | solution.py:14
  108.1 6.2 %gather_fusion = bf16[384,64,64]{2,1,0:T(8,128)(2,1)} fusion(bf16[64,256,64]{2,0,1:T(8,128)(2,1)} %bitcast.61, s32[1024]{0:T(1024)S(1)} %pad_clamp_fusion), kind=kCustom, calls=%fused_computation.clone | custom fusion | bytes 6292992 | tf_op jit(solution)/shard_map/jit(_take)/gather | solution.py:14
  114.3 43.4 %all-gather.8.cloned.1.call-done = bf16[384,4096]{1,0:T(8,128)(2,1)} async-done(((bf16[24,4096]{1,0:T(8,128)(2,1)}), bf16[384,4096]{1,0:T(8,128)(2,1)}) %all-gather.8.cloned.1.call-update) | async-done | bytes 3145744 | tf_op jit(solution)/shard_map/all_gather | solution.py:51
  157.6 3.4 %copy.20 = bf16[384,4096]{0,1:T(8,128)(2,1)S(1)} copy(bf16[384,4096]{1,0:T(8,128)(2,1)} %all-gather.8.cloned.1.call-done) | data formatting | bytes 6291456 | tf_op jit(solution)/shard_map/all_gather | solution.py:51
  161.1 9.5 %copy.21 = bf16[384,64,64]{2,1,0:T(8,128)(2,1)} copy(bf16[384,64,64]{0,2,1:T(8,128)(2,1)S(1)} %bitcast.62) | data formatting | bytes 6291456 | tf_op jit(solution)/shard_map/reshape | solution.py:13
  170.5 12.6 %fusion.1 = f32[384,64,64]{2,1,0:T(8,128)} fusion(bf16[384,64,64]{2,1,0:T(8,128)(2,1)} %copy.21, bf16[384,64,64]{2,1,0:T(8,128)(2,1)} %gather_fusion.1, pred[384]{0:T(512)(128)(4,1)S(1)} %compare_and_fusion), kind=kOutput, calls=%fused_computation.4 | convolution fusion | flops 202899456 | bytes 12583296 | tf_op jit(solution)/shard_map/pij,sopj->psoi/dot_general | solution.py:15
  183.1 11.4 %copy.26 = f32[384,64,64]{0,2,1:T(8,128)} copy(f32[384,64,64]{2,1,0:T(8,128)} %fusion.1) | data formatting | bytes 12582912 | tf_op jit(solution)/shard_map/pij,sopj->psoi/dot_general | solution.py:15
  194.5 3.5 %fusion.6 = (bf16[384,4096]{0,1:T(8,128)(2,1)S(1)}, bf16[384,4096]{0,1:T(8,128)(2,1)S(1)}) fusion(f32[384,64,64]{0,2,1:T(8,128)} %copy.26), kind=kLoop, calls=%fused_computation.10 | loop fusion | flops 6291456 | bytes 12582912 | tf_op jit(solution)/shard_map/convert_element_type | solution.py:18
  198.0 0.9 fusion.14
  198.9 0.9 fusion.11
  199.8 0.3 convert_element_type.69
  200.1 0.2 copy.27
  200.3 0.9 convert_element_type.71
  201.1 12.6 %fusion.4 = f32[384,64,64]{2,1,0:T(8,128)} fusion(bf16[384,64,64]{2,1,0:T(8,128)(2,1)} %copy.21, bf16[384,64,64]{2,1,0:T(8,128)(2,1)} %gather_fusion, pred[384]{0:T(512)(128)(4,1)S(1)} %compare_and_fusion), kind=kOutput, calls=%fused_computation.7 | convolution fusion | flops 202899456 | bytes 12583296 | tf_op jit(solution)/shard_map/pij,sopj->psoi/dot_general | solution.py:15
  213.7 11.4 %copy.22 = f32[384,64,64]{0,2,1:T(8,128)} copy(f32[384,64,64]{2,1,0:T(8,128)} %fusion.4) | data formatting | bytes 12582912 | tf_op jit(solution)/shard_map/pij,sopj->psoi/dot_general | solution.py:15
  225.1 3.5 %fusion.7 = (bf16[384,4096]{0,1:T(8,128)(2,1)S(1)}, bf16[384,4096]{0,1:T(8,128)(2,1)S(1)}) fusion(f32[384,64,64]{0,2,1:T(8,128)} %copy.22), kind=kLoop, calls=%fused_computation.13 | loop fusion | flops 6291456 | bytes 12582912 | tf_op jit(solution)/shard_map/convert_element_type | solution.py:18
  228.6 0.9 fusion.15
  229.5 0.9 fusion.10
  230.4 0.3 convert_element_type.62
  230.7 0.2 copy.23
  230.9 0.9 convert_element_type.64
  (6 shorter events, 0.0 us)
Async XLA Ops:
  7.2 43.1 %all-gather.10.cloned.1.call-start = ((), (), s32[]{:S(2)}) async-start(), calls=%async_computation.2 | async-start | bytes 2228224 | tf_op jit(solution)/shard_map/all_gather | solution.py:40
  7.9 80.4 %all-gather.6.cloned.1.call-start = ((), (), s32[]{:S(2)}) async-start(), calls=%async_computation | async-start | bytes 2228224 | tf_op jit(solution)/shard_map/all_gather | solution.py:39
  8.6 149.0 %all-gather.8.cloned.1.call-start = ((), (), s32[]{:S(2)}) async-start(), calls=%async_computation.1 | async-start | bytes 3342336 | tf_op jit(solution)/shard_map/all_gather | solution.py:51
Sparse Core Ops, SparseCore 0:
  9.8 40.4 all-gather.9
  52.1 36.1 all-gather.5
  90.7 66.8 all-gather.7
where the time goes:
time: 239 us; the launch traced here: 238 us
  waiting for transfers between devices  87.1 us (36%)
  local copies, waits for them, and re-layouts  80.3 us (34%)
  matrix products  28.8 us (12%)
  blocking collectives  18.1 us (8%)
  between operations  15.1 us (6%)
  other arithmetic  8.74 us (4%)
    all_gather x1, waiting for transfers between devices, local(): lax.all_gather(tile_flat, 'col', axis=0, tiled=True)  43.4 us
    dot_general x2, matrix products, make_folder(): jnp.einsum('pij,sopj->psoi', tile_mats, picked, preferred_element_type=jn...  25.1 us
    all_gather x1, waiting for transfers between devices, local(): lax.all_gather(coefs, 'row', axis=1, tiled=True)  24.6 us
    dot_general x2, local copies, waits for them, and re-layouts, make_folder(): jnp.einsum('pij,sopj->psoi', tile_mats, picked, preferred_element_type=jn...  22.7 us
    all_gather x1, blocking collectives, local(): lax.all_gather(cols_global, 'col', axis=0, tiled=True)  18.1 us
    all_gather x1, waiting for transfers between devices, local(): lax.all_gather(direction, 'row', axis=1, tiled=True)  17.7 us
    reshape x2, local copies, waits for them, and re-layouts, local(): coef_panel = whole_coefs.reshape(1, orbitals, all_blocks, BLOCK)  13.4 us
    reshape x2, local copies, waits for them, and re-layouts, local(): direction_panel = whole_direction.reshape(1, orbitals, all_blocks, BLOCK)  13.3 us
  transfers between devices with their start and end apart: 3, of which 3 were waited for; matrix products, arithmetic and copies ran while one was open for 18% of the time, Pallas kernels for 0%

commit v1 on v0

--- a/solution.py
+++ b/solution.py
@@ -27,6 +27,19 @@
 
 
 def local(coefs, direction, tiles, block_rows, block_cols, counts):
+
+    def carry_words(matrix, mesh_name):
+        current_block = jnp.concatenate(
+            lax.all_to_all(
+                jnp.stack([matrix for _ in range(lax.psum(1, axis_name=mesh_name))]),
+                axis_name=mesh_name,
+                concat_axis=0,
+                split_axis=0,
+            ),
+            axis=1,
+        )
+        return current_block
+
     slots = tiles.shape[1]
     orbitals = coefs.shape[0]
     row_blocks = coefs.shape[1] // BLOCK
@@ -37,7 +50,7 @@
     cols_global = block_cols[0]
     whole_coefs, whole_direction = (
         lax.all_gather(coefs, "row", axis=1, tiled=True),
-        lax.all_gather(direction, "row", axis=1, tiled=True),
+        carry_words(direction, "row"),
     )
     all_blocks = whole_coefs.shape[1] // BLOCK
     coef_panel = whole_coefs.reshape(1, orbitals, all_blocks, BLOCK)

time: 239 us -> 217 us (0.908)
  waiting for transfers between devices: 87.1 us -> 39.6 us
  blocking collectives: 18.1 us -> 33.6 us
  starting transfers between devices: 0.11 us -> 7.23 us
    all_gather x1, waiting for transfers between devices: 24.6 us -> 0.01 us  [local(): lax.all_gather(coefs, 'row', axis=1, tiled=True)]
    all_gather x1 -> x0, waiting for transfers between devices: 17.7 us -> none  [local(): lax.all_gather(direction, 'row', axis=1, tiled=True)]
    all_gather x1, blocking collectives: 18.1 us -> 33.6 us  [local(): lax.all_gather(cols_global, 'col', axis=0, tiled=True)]
    another operation x0 -> x3, local copies, waits for them, and re-layouts: none -> 13.3 us  [the longest x2 10.8 us: local(): direction_panel = whole_direction.reshape(1, orbitals, all_blocks, BLOCK)]
    reshape x2 -> x1, local copies, waits for them, and re-layouts: 13.3 us -> 2.78 us  [carry_words(): jnp.concatenate(lax.all_to_all(jnp.stack([matrix for _ in range(lax.psum(...]
    all_to_all x0 -> x1, starting transfers between devices: none -> 7.16 us  [carry_words(): lax.all_to_all(jnp.stack([matrix for _ in range(lax.psum(1, axis_name=mes...]
    all_gather x1, waiting for transfers between devices: 43.4 us -> 38.7 us  [local(): lax.all_gather(tile_flat, 'col', axis=0, tiled=True)]
  transfers between devices with their start and end apart: 3 -> 3, of which waited for: 3 -> 2; matrix products, arithmetic and copies ran while one was open for 18% -> 21% of each run, Pallas kernels for 0% -> 0%
where the time goes in v1:
time: 217 us; the launch traced here: 216 us
  local copies, waits for them, and re-layouts  82.3 us (38%)
  waiting for transfers between devices  39.6 us (18%)
  blocking collectives  33.6 us (15%)
  matrix products  28.8 us (13%)
  between operations  15.4 us (7%)
  other arithmetic  8.74 us (4%)
  starting transfers between devices  7.23 us (3%)
    all_gather x1, waiting for transfers between devices, local(): lax.all_gather(tile_flat, 'col', axis=0, tiled=True)  38.7 us
    all_gather x1, blocking collectives, local(): lax.all_gather(cols_global, 'col', axis=0, tiled=True)  33.6 us
    dot_general x2, matrix products, make_folder(): jnp.einsum('pij,sopj->psoi', tile_mats, picked, preferred_element_type=jn...  25.1 us
    dot_general x2, local copies, waits for them, and re-layouts, make_folder(): jnp.einsum('pij,sopj->psoi', tile_mats, picked, preferred_element_type=jn...  22.7 us
    reshape x2, local copies, waits for them, and re-layouts, local(): coef_panel = whole_coefs.reshape(1, orbitals, all_blocks, BLOCK)  13.4 us
    gather x2, local copies, waits for them, and re-layouts, make_folder(): picked = jnp.take(panels, tile_cols, axis=2)  12.4 us
    another operation x2, local copies, waits for them, and re-layouts, local(): direction_panel = whole_direction.reshape(1, orbitals, all_blocks, BLOCK)  10.8 us
    reshape x1, local copies, waits for them, and re-layouts, make_folder(): tile_mats = tile_flat.reshape(amount, BLOCK, BLOCK)  9.49 us
  transfers between devices with their start and end apart: 3, of which 2 were waited for; matrix products, arithmetic and copies ran while one was open for 21% of the time, Pallas kernels for 0%

profile of v1, /device:TPU:1, one launch (start us, length us, event | category | flops | bytes accessed | tf_op | source)
XLA Modules:
  0.0 215.7 jit_solution(16712276679226359656)
XLA Ops:
  7.2 0.0 copy-start.3
  7.2 0.0 copy-start.1
  7.2 0.0 copy-start.2
  7.2 0.0 all-gather.5.cloned.1.call-start
  7.2 0.7 all-gather.5.cloned.1.call-update
  7.9 0.0 all-gather.7.cloned.1.call-start
  8.6 1.7 bitcast_multiply_fusion
  10.3 0.0 all-gather.7.cloned.1.call-update
  10.3 2.5 %stack.2 = bf16[16,64,1024]{2,1,0:T(8,128)(2,1)} broadcast(bf16[64,1024]{1,0:T(8,128)(2,1)} %param.9), dimensions={1,2} | broadcast | bytes 2228224 | tf_op jit(solution)/shard_map/stack | solution.py:34
  12.8 7.2 %all-to-all-start = ((bf16[16,64,1024]{2,1,0:T(8,128)(2,1)}), bf16[16,64,1024]{2,1,0:T(8,128)(2,1)S(1)}, u32[]{:S(2)}, u32[]{:S(2)}) async-start(bf16[16,64,1024]{2,1,0:T(8,128)(2,1)} %stack.2), calls=%async_computation | async-start | bytes 4194304 | tf_op jit(solution)/shard_map/all_to_all | solution.py:33
  20.0 0.0 copy-done.3
  20.0 0.6 dynamic-slice
  21.3 0.0 copy-done.1
  21.3 0.1 bitcast_dynamic-update-slice_fusion
  21.4 0.0 copy-done.2
  21.4 0.1 bitcast_dynamic-update-slice_fusion.1
  21.5 33.6 %all-reduce.2 = (s32[384]{0:T(512)S(1)}, s32[384]{0:T(512)S(1)}) all-reduce(s32[384]{0:T(512)S(1)} %bitcast_dynamic-update-slice_fusion, s32[384]{0:T(512)S(1)} %bitcast_dynamic-update-slice_fusion.1), channel_id=3, replica_groups=mesh['row'=16,'col'=16] {'col'}, use_global_device_ids=true, to_apply=%add.1 | all-reduce | flops 768 | bytes 6144 | tf_op jit(solution)/shard_map/all_gather | solution.py:66
  55.1 0.3 all-to-all-done
  55.3 0.0 copy-start
  55.3 1.3 copy-done
  56.7 2.8 %copy.24 = bf16[64,16,1024]{2,1,0:T(8,128)(2,1)S(1)} copy(bf16[64,16,1024]{2,0,1:T(8,128)(2,1)} %bitcast.64) | data formatting | bytes 4194304 | tf_op jit(solution)/shard_map/reshape | solution.py:32
  59.4 4.0 %reshape_reshape.3 = bf16[1,64,256,64]{3,2,1,0:T(8,128)(2,1)} reshape(bf16[64,16,1024]{2,1,0:T(8,128)(2,1)S(1)} %copy.24) | data formatting | bytes 4194304 | tf_op jit(solution)/shard_map/reshape;reshape | solution.py:57
  63.4 6.8 %copy.31 = bf16[1,64,256,64]{3,1,2,0:T(8,128)(2,1)} copy(bf16[1,64,256,64]{3,2,1,0:T(8,128)(2,1)} %reshape_reshape.3) | data formatting | bytes 4194304 | tf_op jit(solution)/shard_map/reshape;reshape | solution.py:57
  70.3 0.0 all-gather.5.cloned.1.call-done
  70.3 6.5 %reshape.67 = bf16[1,64,256,64]{3,2,1,0:T(8,128)(2,1)} reshape(bf16[64,16384]{1,0:T(8,128)(2,1)} %all-gather.5.cloned.1.call-done) | data formatting | bytes 4194304 | tf_op jit(solution)/shard_map/reshape | solution.py:56
  76.8 6.9 %copy.32 = bf16[1,64,256,64]{3,1,2,0:T(8,128)(2,1)} copy(bf16[1,64,256,64]{3,2,1,0:T(8,128)(2,1)} %reshape.67) | data formatting | bytes 4194304 | tf_op jit(solution)/shard_map/reshape | solution.py:56
  83.7 6.3 %gather_fusion.1 = bf16[384,64,64]{2,1,0:T(8,128)(2,1)} fusion(bf16[64,256,64]{2,0,1:T(8,128)(2,1)} %bitcast.61, s32[1024]{0:T(1024)S(1)} %pad_clamp_fusion), kind=kCustom, calls=%fused_computation.1.clone | custom fusion | bytes 6292992 | tf_op jit(solution)/shard_map/jit(_take)/gather | solution.py:14
  89.9 6.1 %gather_fusion = bf16[384,64,64]{2,1,0:T(8,128)(2,1)} fusion(bf16[64,256,64]{2,0,1:T(8,128)(2,1)} %bitcast.62, s32[1024]{0:T(1024)S(1)} %pad_clamp_fusion), kind=kCustom, calls=%fused_computation.clone | custom fusion | bytes 6292992 | tf_op jit(solution)/shard_map/jit(_take)/gather | solution.py:14
  96.1 38.7 %all-gather.7.cloned.1.call-done = bf16[384,4096]{1,0:T(8,128)(2,1)} async-done(((bf16[24,4096]{1,0:T(8,128)(2,1)}), bf16[384,4096]{1,0:T(8,128)(2,1)}) %all-gather.7.cloned.1.call-update) | async-done | bytes 3145744 | tf_op jit(solution)/shard_map/all_gather | solution.py:64
  134.8 3.4 %copy.20 = bf16[384,4096]{0,1:T(8,128)(2,1)S(1)} copy(bf16[384,4096]{1,0:T(8,128)(2,1)} %all-gather.7.cloned.1.call-done) | data formatting | bytes 6291456 | tf_op jit(solution)/shard_map/all_gather | solution.py:64
  138.2 9.5 %copy.21 = bf16[384,64,64]{2,1,0:T(8,128)(2,1)} copy(bf16[384,64,64]{0,2,1:T(8,128)(2,1)S(1)} %bitcast.63) | data formatting | bytes 6291456 | tf_op jit(solution)/shard_map/reshape | solution.py:13
  147.7 12.6 %fusion.1 = f32[384,64,64]{2,1,0:T(8,128)} fusion(bf16[384,64,64]{2,1,0:T(8,128)(2,1)} %copy.21, bf16[384,64,64]{2,1,0:T(8,128)(2,1)} %gather_fusion.1, pred[384]{0:T(512)(128)(4,1)S(1)} %compare_and_fusion), kind=kOutput, calls=%fused_computation.4 | convolution fusion | flops 202899456 | bytes 12583296 | tf_op jit(solution)/shard_map/pij,sopj->psoi/dot_general | solution.py:15
  160.3 11.4 %copy.27 = f32[384,64,64]{0,2,1:T(8,128)} copy(f32[384,64,64]{2,1,0:T(8,128)} %fusion.1) | data formatting | bytes 12582912 | tf_op jit(solution)/shard_map/pij,sopj->psoi/dot_general | solution.py:15
  171.6 3.5 %fusion.6 = (bf16[384,4096]{0,1:T(8,128)(2,1)S(1)}, bf16[384,4096]{0,1:T(8,128)(2,1)S(1)}) fusion(f32[384,64,64]{0,2,1:T(8,128)} %copy.27), kind=kLoop, calls=%fused_computation.10 | loop fusion | flops 6291456 | bytes 12582912 | tf_op jit(solution)/shard_map/convert_element_type | solution.py:18
  175.1 0.9 fusion.14
  176.0 0.9 fusion.11
  177.0 0.3 convert_element_type.69
  177.2 0.2 copy.28
  177.4 0.9 convert_element_type.71
  178.3 12.6 %fusion.4 = f32[384,64,64]{2,1,0:T(8,128)} fusion(bf16[384,64,64]{2,1,0:T(8,128)(2,1)} %copy.21, bf16[384,64,64]{2,1,0:T(8,128)(2,1)} %gather_fusion, pred[384]{0:T(512)(128)(4,1)S(1)} %compare_and_fusion), kind=kOutput, calls=%fused_computation.7 | convolution fusion | flops 202899456 | bytes 12583296 | tf_op jit(solution)/shard_map/pij,sopj->psoi/dot_general | solution.py:15
  190.8 11.4 %copy.22 = f32[384,64,64]{0,2,1:T(8,128)} copy(f32[384,64,64]{2,1,0:T(8,128)} %fusion.4) | data formatting | bytes 12582912 | tf_op jit(solution)/shard_map/pij,sopj->psoi/dot_general | solution.py:15
  202.2 3.5 %fusion.7 = (bf16[384,4096]{0,1:T(8,128)(2,1)S(1)}, bf16[384,4096]{0,1:T(8,128)(2,1)S(1)}) fusion(f32[384,64,64]{0,2,1:T(8,128)} %copy.22), kind=kLoop, calls=%fused_computation.13 | loop fusion | flops 6291456 | bytes 12582912 | tf_op jit(solution)/shard_map/convert_element_type | solution.py:18
  205.7 0.9 fusion.15
  206.7 0.9 fusion.10
  207.6 0.3 convert_element_type.62
  207.8 0.2 copy.23
  208.0 0.9 convert_element_type.64
  (6 shorter events, 0.0 us)
Async XLA Ops:
  7.2 12.8 %copy-start.3 = (u32[256]{0:T(256)S(1)}, u32[256]{0:T(256)}, u32[]{:S(2)}) copy-start(u32[256]{0:T(256)} %constant.16) | copy-start | bytes 3076
  7.2 14.1 %copy-start.1 = (s32[1,24]{1,0:T(1,128)S(1)}, s32[1,24]{1,0:T(1,128)}, u32[]{:S(2)}) copy-start(s32[1,24]{1,0:T(1,128)} %param.12) | copy-start | bytes 292
  7.2 14.2 %copy-start.2 = (s32[1,24]{1,0:T(1,128)S(1)}, s32[1,24]{1,0:T(1,128)}, u32[]{:S(2)}) copy-start(s32[1,24]{1,0:T(1,128)} %param.11) | copy-start | bytes 292
  7.2 63.1 %all-gather.5.cloned.1.call-start = ((), (), s32[]{:S(2)}) async-start(), calls=%async_computation.1 | async-start | bytes 2228224 | tf_op jit(solution)/shard_map/all_gather | solution.py:52
  7.9 126.8 %all-gather.7.cloned.1.call-start = ((), (), s32[]{:S(2)}) async-start(), calls=%async_computation.2 | async-start | bytes 3342336 | tf_op jit(solution)/shard_map/all_gather | solution.py:64
  12.8 42.5 %all-to-all-start = ((bf16[16,64,1024]{2,1,0:T(8,128)(2,1)}), bf16[16,64,1024]{2,1,0:T(8,128)(2,1)S(1)}, u32[]{:S(2)}, u32[]{:S(2)}) async-start(bf16[16,64,1024]{2,1,0:T(8,128)(2,1)} %stack.2), calls=%async_computation | async-start | bytes 4194304 | tf_op jit(solution)/shard_map/all_to_all | solution.py:33
  55.3 1.3 copy-start
Sparse Core Ops, SparseCore 0:
  9.8 54.1 all-gather.4
  66.5 68.2 all-gather.6
